TPU v7x, 32 devices: a whole 2x2x4 slice. The times are simulated.
32 devices in a mesh: center: 8 (over z, y), rep: 4 (over x, core).
Axes of the slice: x: 2, y: 2, z: 4, core: 2. Of those that a mesh axis runs over, the one named last changes fastest.
Arguments:
- faces: bfloat16 [2048, 512], P(('center', 'rep')), may hold values from -1800 to 1800
- w_first: bfloat16 [512, 512], replicated, may hold values from -1.1 to 1.1
- w_second: bfloat16 [512, 512], replicated, may hold values from -1.1 to 1.1
- gain_first: float32 [512], replicated, may hold values from 0.46 to 1.54
- bias_first: float32 [512], replicated, may hold values from -3 to 3
- gain_second: float32 [512], replicated, may hold values from 0.46 to 1.54
- centers: float32 [16384, 512], P('center'), may hold values from -6 to 6
- momentum: float32 [16384, 512], P('center'), may hold values from -1.2 to 1.2
- sample_index: int32 [1024], P('center'), may hold values from 0 to 2047, as said below
- live_count: int32 [8], P('center'), may hold values from 16 to 128, as said below
- labels: int32 [2048], P(('center', 'rep')), may hold values from 0 to 1023, as said below
Outputs:
- loss: float32 [2048], P(('center', 'rep'))
- feat_grad: float32 [2048, 512], P(('center', 'rep'))
- new_centers: float32 [1024, 512], P('center')
- new_momentum: float32 [1024, 512], P('center')
Inputs may be any that keep to these rules, and one draw needn't show every extreme that they name: `sample_index`: the 128 entries of one shard are distinct rows of that shard. The live slots of a shard are its first live_count entries; some shard has 128 of them and some shard 128 // 8. `labels`: each label is a live sampled slot, counted over all shards' lists in shard order.
All inputs are finite; a program needn't handle non-finite values.
Results may differ from a plain program's by a relative error of at most 0.0075.
Values may be sent and summed in bfloat16 or wider, within the bound.
No kernel may reach another device: no remote copies, remote signals or barrier semaphores. Data moves between devices by JAX's collectives and lax.ppermute only.
A program may use at most 64 MiB of HBM per device.

v0:
```python
import jax
import jax.numpy as jnp
from jax import lax
from jax.sharding import PartitionSpec as P

LOGIT_SCALE = 64.0
COS_MARGIN = 0.35
LEARN_RATE = 0.5
MOMENT_COEF = 0.9
DECAY_COEF = 0.0005
NORM_EPS = 1e-05
LENGTH_EPS = 1e-06


def batch_norm(values, gain_vec, sample_count):
    summed, squares = lax.psum((jnp.sum(values, 0), jnp.sum(values * values, 0)), "rep")
    mean_vec = summed / sample_count
    spread = squares / sample_count - mean_vec * mean_vec
    return gain_vec * (values - mean_vec) * lax.rsqrt(spread + NORM_EPS)


def momentum_step(raw_grad, picked, center_len, center_unit, picked_momentum, live_slot):
    center_radial = jnp.sum(center_unit * raw_grad, 1, keepdims=True)
    center_grad = (raw_grad - center_unit * center_radial) / center_len
    velocity = MOMENT_COEF * picked_momentum + center_grad + DECAY_COEF * picked
    velocity = jnp.where(live_slot[:, None], velocity, picked_momentum)
    placed = jnp.where(live_slot[:, None], picked - LEARN_RATE * velocity, picked)
    return (placed, velocity)


def per_device(
    faces,
    w_first,
    w_second,
    gain_first,
    bias_first,
    gain_second,
    centers,
    momentum,
    sample_index,
    live_count,
    labels,
):
    face_rows = faces.shape[0]
    width = faces.shape[1]
    sample_count = face_rows * lax.axis_size("rep")
    first_out = jnp.dot(faces, w_first, preferred_element_type=jnp.float32)
    hidden = jnp.maximum(batch_norm(first_out, gain_first, sample_count) + bias_first, 0.0).astype(
        jnp.bfloat16
    )
    second = jnp.dot(hidden, w_second, preferred_element_type=jnp.float32)
    feature = batch_norm(second, gain_second, sample_count)
    length = jnp.sqrt(jnp.sum(feature * feature, 1, keepdims=True) + LENGTH_EPS)
    unit_rows = feature / length
    unit_low = unit_rows.astype(jnp.bfloat16)
    all_units, all_labels = (
        lax.all_gather(unit_low, "center", axis=0, tiled=True),
        lax.all_gather(labels, "center", axis=0, tiled=True),
    )
    my_shard = lax.axis_index("center")
    picked = jnp.take(centers, sample_index, axis=0)
    picked_momentum = jnp.take(momentum, sample_index, axis=0)
    center_len = jnp.sqrt(jnp.sum(picked * picked, 1, keepdims=True) + LENGTH_EPS)
    center_unit = picked / center_len
    center_low = center_unit.astype(jnp.bfloat16)
    slot_count = picked.shape[0]
    slot_ids = jnp.arange(slot_count, dtype=jnp.int32)
    live_slot = slot_ids < live_count[0]
    first_slot = my_shard * slot_count
    group_rows = all_units.shape[0]
    block_rows = min(1024, group_rows)
    block_total_count = group_rows // block_rows
    unit_blocks = all_units.reshape(block_total_count, block_rows, width)
    mark_blocks = all_labels.reshape(block_total_count, block_rows)

    def target_of(mark_block):
        return (mark_block - first_slot)[:, None] == slot_ids[None, :]

    def partials(element):
        cosine = jnp.einsum("fd,sd->fs", element[0], center_low, preferred_element_type=jnp.float32)
        target = target_of(element[1])
        logits = LOGIT_SCALE * (cosine - COS_MARGIN * target.astype(jnp.float32))
        exponent = jnp.where(live_slot[None, :], jnp.exp(logits), 0.0)
        return (exponent, jnp.sum(exponent, 1), jnp.sum(jnp.where(target, logits, 0.0), 1))

    exponent_blocks, local_total, local_target = lax.map(partials, (unit_blocks, mark_blocks))
    softmax_total, target_logit = lax.psum(
        (local_total.reshape(group_rows), local_target.reshape(group_rows)), "center"
    )
    group_loss = jnp.log(softmax_total) - target_logit
    loss = lax.dynamic_slice_in_dim(group_loss, my_shard * face_rows, face_rows, 0)
    total_blocks = softmax_total.reshape(block_total_count, block_rows)

    def grad_weight(exponent, mark_block, block_total):
        target = target_of(mark_block)
        return (
            LOGIT_SCALE * (exponent / block_total[:, None] - target.astype(jnp.float32))
        ).astype(jnp.bfloat16)

    start_sum = jnp.zeros((slot_count, width), jnp.float32)

    def both_block(running, element):
        weight = grad_weight(element[2], element[1], element[3])
        running = running + jnp.einsum(
            "fs,fd->sd", weight, element[0], preferred_element_type=jnp.float32
        )
        return (running, jnp.dot(weight, center_low, preferred_element_type=jnp.float32))

    center_raw, unit_terms = lax.scan(
        both_block, start_sum, (unit_blocks, mark_blocks, exponent_blocks, total_blocks)
    )
    unit_grad = lax.psum_scatter(
        unit_terms.reshape(group_rows, width), "center", scatter_dimension=0, tiled=True
    )
    radial = jnp.sum(unit_rows * unit_grad, 1, keepdims=True)
    feat_grad = (unit_grad - unit_rows * radial) / length
    raw_grad = lax.psum(center_raw, "rep")
    new_centers, new_momentum = momentum_step(
        raw_grad, picked, center_len, center_unit, picked_momentum, live_slot
    )
    return (loss, feat_grad, new_centers, new_momentum)


def solution(mesh):
    return jax.shard_map(
        per_device,
        mesh=mesh,
        in_specs=(
            P(("center", "rep"), None),
            P(),
            P(),
            P(),
            P(),
            P(),
            P("center", None),
            P("center", None),
            P("center"),
            P("center"),
            P(("center", "rep")),
        ),
        out_specs=(
            P(("center", "rep")),
            P(("center", "rep"), None),
            P("center", None),
            P("center", None),
        ),
        check_vma=False,
    )
```

profile of v0, /device:TPU:0, one launch (start us, length us, event | category | flops | bytes accessed | tf_op | source)
XLA Modules:
  0.0 172.2 jit_solution(15847876268697771019)
XLA Ops:
  8.0 0.0 copy-start
  8.0 0.0 all-reduce.6.cloned.1.call-start
  8.8 0.7 compare_select_fusion
  9.4 0.7 compare_and_fusion
  10.1 1.2 dynamic-slice.4
  12.0 0.9 dynamic-update-slice
  12.8 13.1 %all-reduce = s32[512]{0:T(512)S(1)} all-reduce(s32[512]{0:T(512)S(1)} %dynamic-update-slice), channel_id=1, replica_groups=mesh['center'=8,'rep'=4] {'center'}, use_global_device_ids=true, to_apply=%add | all-reduce | flops 512 | bytes 4096
  25.9 0.0 copy-done
  25.9 1.1 fusion.16
  27.0 5.7 %all-reduce.3 = (f32[512]{0:T(512)S(1)}, f32[512]{0:T(512)S(1)}) all-reduce(f32[512]{0:T(512)S(1)} %get-tuple-element.60, f32[512]{0:T(512)S(1)} %get-tuple-element.49), channel_id=1, replica_groups=mesh['center'=8,'rep'=4] {'rep'}, use_global_device_ids=true, to_apply=%region_3.0 | all-reduce | flops 1024 | bytes 8192 | tf_op jit(solution)/shard_map/psum | solution.py:16
  32.7 1.3 fusion.15
  34.0 6.6 %all-reduce.2 = (f32[512]{0:T(512)S(1)}, f32[512]{0:T(512)S(1)}) all-reduce(f32[512]{0:T(512)S(1)} %get-tuple-element.48, f32[512]{0:T(512)S(1)} %get-tuple-element.47), channel_id=1, replica_groups=mesh['center'=8,'rep'=4] {'rep'}, use_global_device_ids=true, to_apply=%region_7.0 | all-reduce | flops 1024 | bytes 8192 | tf_op jit(solution)/shard_map/psum | solution.py:16
  40.6 0.8 multiply_reduce_fusion.3
  41.5 0.8 fusion.13
  42.2 3.1 %gather_fusion = f32[128,512]{1,0:T(8,128)S(1)} fusion(f32[2048,512]{1,0:T(8,128)} %param.19, s32[1024]{0:T(1024)S(1)} %pad_clamp_fusion), kind=kCustom, calls=%fused_computation.clone | custom fusion | bytes 524800 | tf_op jit(solution)/shard_map/jit(_take)/gather | solution.py:61
  45.3 0.2 multiply_reduce_fusion.1
  45.5 31.2 %all_gather.6 = bf16[512,512]{1,0:T(8,128)(2,1)S(1)} all-gather(bf16[64,512]{1,0:T(8,128)(2,1)S(1)} %fusion.13), channel_id=1, replica_groups=mesh['center'=8,'rep'=4] {'center'}, dimensions={0}, use_global_device_ids=true | all-gather | bytes 589824 | tf_op jit(solution)/shard_map/all_gather | solution.py:57
  76.7 0.4 fusion.1
  77.1 18.9 %all-reduce.1 = (f32[512]{0:T(512)S(1)}, f32[512]{0:T(512)S(1)}) all-reduce(f32[512]{0:T(512)S(1)} %get-tuple-element.46, f32[512]{0:T(512)S(1)} %get-tuple-element.45), channel_id=1, replica_groups=mesh['center'=8,'rep'=4] {'center'}, use_global_device_ids=true, to_apply=%region_13.15 | all-reduce | flops 1024 | bytes 8192 | tf_op jit(solution)/shard_map/psum | solution.py:87
  96.0 1.0 fusion.14
  97.0 0.0 copy-start.1
  97.0 0.0 all-reduce.6.cloned.1.call-update
  97.1 0.0 reduce-scatter.2.cloned.1.call-start
  97.1 1.4 fusion.4
  98.5 0.0 reduce-scatter.2.cloned.1.call-update
  98.5 3.1 %gather_fusion.1 = f32[128,512]{1,0:T(8,128)S(1)} fusion(f32[2048,512]{1,0:T(8,128)} %param.20, s32[1024]{0:T(1024)S(1)} %pad_clamp_fusion), kind=kCustom, calls=%fused_computation.1.clone | custom fusion | bytes 524800 | tf_op jit(solution)/shard_map/jit(_take)/gather | solution.py:62
  101.6 0.6 dynamic_slice.19
  102.2 23.7 %all-reduce.6.cloned.1.call-done = f32[128,512]{1,0:T(8,128)} async-done(((f32[128,512]{1,0:T(8,128)}), f32[128,512]{1,0:T(8,128)}) %all-reduce.6.cloned.1.call-update) | async-done | bytes 262160 | tf_op jit(solution)/shard_map/psum | solution.py:117
  126.0 1.1 multiply_reduce_fusion
  127.1 1.9 %subtract_select_fusion = (f32[128,512]{1,0:T(8,128)}, f32[128,512]{1,0:T(8,128)}) fusion(f32[128,512]{1,0:T(8,128)S(1)} %gather_fusion, pred[128]{0:T(512)(128)(4,1)S(1)} %get-tuple-element.86, pred[128]{0:T(512)(128)(4,1)S(1)} %get-tuple-element.87, f32[128,512]{1,0:T(8,128)} %all-reduce.6.cloned.1.call-done, f32[128]{0:T(128)S(1)} %multiply_reduce_fusion, ...), kind=kLoop, calls=%fused_computation.4 | loop fusion | flops 917504 | bytes 1312000 | tf_op jit(solution)/shard_map/jit(_where)/select_n | solution.py:27
  129.1 33.0 %reduce-scatter.2.cloned.1.call-done = f32[64,512]{1,0:T(8,128)} async-done(((f32[512,512]{1,0:T(8,128)}), f32[64,512]{1,0:T(8,128)}) %reduce-scatter.2.cloned.1.call-update) | async-done | bytes 131088 | tf_op jit(solution)/shard_map/reduce_scatter | solution.py:112
  162.0 0.0 copy-done.1
  162.0 1.1 multiply_reduce_fusion.2
  163.1 1.7 subtract_divide_fusion
  (8 shorter events, 0.1 us)
Async XLA Ops:
  8.0 17.9 %copy-start = (bf16[512,512]{1,0:T(8,128)(2,1)S(1)}, bf16[512,512]{1,0:T(8,128)(2,1)}, u32[]{:S(2)}) copy-start(bf16[512,512]{1,0:T(8,128)(2,1)} %param.14) | copy-start | bytes 1572868
  8.0 118.0 %all-reduce.6.cloned.1.call-start = ((), (), s32[]{:S(2)}) async-start(), calls=%async_computation.2 | async-start | bytes 524288 | tf_op jit(solution)/shard_map/psum | solution.py:117
  97.0 65.0 %copy-start.1 = (f32[512]{0:T(512)S(1)}, f32[512]{0:T(512)}, u32[]{:S(2)}) copy-start(f32[512]{0:T(512)} %param.18) | copy-start | bytes 6148
  97.1 65.0 %reduce-scatter.2.cloned.1.call-start = ((), (), s32[]{:S(2)}) async-start(), calls=%async_computation.1 | async-start | bytes 1179648 | tf_op jit(solution)/shard_map/reduce_scatter | solution.py:112
Sparse Core Ops, SparseCore 0:
  97.2 28.7 all-reduce.5
Sparse Core Ops, SparseCore 1:
  100.9 61.0 reduce-scatter.1
where the time goes:
time: 173 us; the launch traced here: 172 us
  blocking collectives  75.5 us (44%)
  waiting for transfers between devices  56.7 us (33%)
  between operations  16.9 us (10%)
  other arithmetic  8.98 us (5%)
  local copies, waits for them, and re-layouts  8.84 us (5%)
  matrix products  5.14 us (3%)
    reduce_scatter x1, waiting for transfers between devices, per_device(): lax.psum_scatter(unit_terms.reshape(group_rows, width), 'center', scatter...  33 us
    all_gather x1, blocking collectives, per_device(): lax.all_gather(unit_low, 'center', axis=0, tiled=True)  31.2 us
    psum x1, waiting for transfers between devices, per_device(): raw_grad = lax.psum(center_raw, 'rep')  23.7 us
    psum x1, blocking collectives, per_device(): lax.psum((local_total.reshape(group_rows), local_target.reshape(group_row...  18.9 us
    unnamed x1, blocking collectives  13.1 us
    psum x2, blocking collectives, batch_norm(): lax.psum((jnp.sum(values, 0), jnp.sum(values * values, 0)), 'rep')  12.3 us
  transfers between devices with their start and end apart: 2, of which 2 were waited for; matrix products, arithmetic and copies ran while one was open for 5% of the time, Pallas kernels for 0%

commit v1 on v0

--- a/solution.py
+++ b/solution.py
@@ -10,6 +10,27 @@
 DECAY_COEF = 0.0005
 NORM_EPS = 1e-05
 LENGTH_EPS = 1e-06
+
+
+def gather_around(shard, axis, dim):
+    size, index, span = (lax.axis_size(axis), lax.axis_index(axis), shard.shape[dim])
+    forward = [(i, (i + 1) % size) for i in range(size)]
+    left = [(i, (i - 1) % size) for i in range(size)]
+    whole = jnp.zeros((*shard.shape[:dim], size * span, *shard.shape[dim + 1 :]), shard.dtype)
+    whole = lax.dynamic_update_slice_in_dim(whole, shard, index * span, axis=dim)
+    from_left = from_right = shard
+    half = size // 2
+    for step in range(1, half + 1):
+        from_left = lax.ppermute(from_left, axis, forward)
+        whole = lax.dynamic_update_slice_in_dim(
+            whole, from_left, (index - step) % size * span, axis=dim
+        )
+        if step < size - half:
+            from_right = lax.ppermute(from_right, axis, left)
+            whole = lax.dynamic_update_slice_in_dim(
+                whole, from_right, (index + step) % size * span, axis=dim
+            )
+    return whole
 
 
 def batch_norm(values, gain_vec, sample_count):
@@ -54,7 +75,7 @@
     unit_rows = feature / length
     unit_low = unit_rows.astype(jnp.bfloat16)
     all_units, all_labels = (
-        lax.all_gather(unit_low, "center", axis=0, tiled=True),
+        gather_around(unit_low, "center", 0),
         lax.all_gather(labels, "center", axis=0, tiled=True),
     )
     my_shard = lax.axis_index("center")

time: 173 us -> 167 us (0.965)
  blocking collectives: 75.5 us -> 41.2 us
  starting transfers between devices: 0.08 us -> 14.5 us
  waiting for transfers between devices: 56.7 us -> 69.9 us
    all_gather x1 -> x0, blocking collectives: 31.2 us -> none  [per_device(): lax.all_gather(unit_low, 'center', axis=0, tiled=True)]
    ppermute x0 -> x7, starting transfers between devices: none -> 14.4 us  [the longest x3 12 us: gather_around(): from_right = lax.ppermute(from_right, axis, left)]
    ppermute x0 -> x7, waiting for transfers between devices: none -> 11.8 us  [the longest x4 11.8 us: gather_around(): from_left = lax.ppermute(from_left, axis, forward)]
    unnamed x1, blocking collectives: 13.1 us -> 9.91 us
    psum x2, blocking collectives: 12.3 us -> 14.1 us  [batch_norm(): lax.psum((jnp.sum(values, 0), jnp.sum(values * values, 0)), 'rep')]
    psum x1, blocking collectives: 18.9 us -> 17.1 us  [per_device(): lax.psum((local_total.reshape(group_rows), local_target.reshape(group_row...]
  transfers between devices with their start and end apart: 2 -> 9, of which waited for: 2 -> 5; matrix products, arithmetic and copies ran while one was open for 5% -> 9% of each run, Pallas kernels for 0% -> 0%
where the time goes in v1:
time: 167 us
  waiting for transfers between devices  69.9 us (42%)
  blocking collectives  41.2 us (25%)
  between operations  17.1 us (10%)
  starting transfers between devices  14.5 us (9%)
  local copies, waits for them, and re-layouts  9.96 us (6%)
  other arithmetic  8.98 us (5%)
  matrix products  5.14 us (3%)
    reduce_scatter x1, waiting for transfers between devices, per_device(): lax.psum_scatter(unit_terms.reshape(group_rows, width), 'center', scatter...  33 us
    psum x1, waiting for transfers between devices, per_device(): raw_grad = lax.psum(center_raw, 'rep')  25 us
    psum x1, blocking collectives, per_device(): lax.psum((local_total.reshape(group_rows), local_target.reshape(group_row...  17.1 us
    psum x2, blocking collectives, batch_norm(): lax.psum((jnp.sum(values, 0), jnp.sum(values * values, 0)), 'rep')  14.1 us
    ppermute x3, starting transfers between devices, gather_around(): from_right = lax.ppermute(from_right, axis, left)  12 us
    ppermute x4, waiting for transfers between devices, gather_around(): from_left = lax.ppermute(from_left, axis, forward)  11.8 us
    unnamed x1, blocking collectives  9.91 us
  transfers between devices with their start and end apart: 9, of which 5 were waited for; matrix products, arithmetic and copies ran while one was open for 9% of the time, Pallas kernels for 0%

profile of v1, /device:TPU:0, one launch (start us, length us, event | category | flops | bytes accessed | tf_op | source)
XLA Modules:
  0.0 166.7 jit_solution(1566686209501540471)
XLA Ops:
  8.0 0.0 copy-start
  8.0 0.0 all-reduce.6.cloned.1.call-start
  8.1 1.0 copy-done
  9.0 1.1 fusion.16
  10.1 8.4 %all-reduce.3 = (f32[512]{0:T(512)S(1)}, f32[512]{0:T(512)S(1)}) all-reduce(f32[512]{0:T(512)S(1)} %get-tuple-element.60, f32[512]{0:T(512)S(1)} %get-tuple-element.49), channel_id=1, replica_groups=mesh['center'=8,'rep'=4] {'rep'}, use_global_device_ids=true, to_apply=%region_3.0 | all-reduce | flops 1024 | bytes 8192 | tf_op jit(solution)/shard_map/psum | solution.py:37
  18.5 1.3 fusion.15
  19.8 5.8 %all-reduce.2 = (f32[512]{0:T(512)S(1)}, f32[512]{0:T(512)S(1)}) all-reduce(f32[512]{0:T(512)S(1)} %get-tuple-element.48, f32[512]{0:T(512)S(1)} %get-tuple-element.47), channel_id=1, replica_groups=mesh['center'=8,'rep'=4] {'rep'}, use_global_device_ids=true, to_apply=%region_7.0 | all-reduce | flops 1024 | bytes 8192 | tf_op jit(solution)/shard_map/psum | solution.py:37
  25.6 0.8 multiply_reduce_fusion.3
  26.5 0.8 constant_dynamic-update-slice_fusion.7
  27.2 1.7 %collective-permute-start = (bf16[64,512]{1,0:T(8,128)(2,1)S(1)}, bf16[64,512]{1,0:T(8,128)(2,1)S(1)}, u32[]{:S(2)}, u32[]{:S(2)}) collective-permute-start(bf16[64,512]{1,0:T(8,128)(2,1)S(1)} %get-tuple-element.80), channel_id=1, source_target_pairs={{0,4},{4,8},{8,12},{12,16},{16,20},{20,24},{24,28},{28,0},{1,5},{5... | collective-permute-start | bytes 196616 | tf_op jit(solution)/shard_map/ppermute | solution.py:24
  28.9 3.1 %collective-permute-start.1 = (bf16[64,512]{1,0:T(8,128)(2,1)S(1)}, bf16[64,512]{1,0:T(8,128)(2,1)S(1)}, u32[]{:S(2)}, u32[]{:S(2)}) collective-permute-start(bf16[64,512]{1,0:T(8,128)(2,1)S(1)} %get-tuple-element.80), channel_id=1, source_target_pairs={{0,28},{4,0},{8,4},{12,8},{16,12},{20,16},{24,20},{28,24},{1,29},{... | collective-permute-start | bytes 196616 | tf_op jit(solution)/shard_map/ppermute | solution.py:29
  32.7 0.7 compare_select_fusion
  33.3 0.7 compare_and_fusion
  34.0 1.2 dynamic-slice.3
  35.9 0.9 dynamic-update-slice
  36.8 9.9 %all-reduce = s32[512]{0:T(512)S(1)} all-reduce(s32[512]{0:T(512)S(1)} %dynamic-update-slice), channel_id=1, replica_groups=mesh['center'=8,'rep'=4] {'center'}, use_global_device_ids=true, to_apply=%add | all-reduce | flops 512 | bytes 4096
  46.7 3.1 %gather_fusion = f32[128,512]{1,0:T(8,128)S(1)} fusion(f32[2048,512]{1,0:T(8,128)} %param.19, s32[1024]{0:T(1024)S(1)} %pad_clamp_fusion), kind=kCustom, calls=%fused_computation.clone | custom fusion | bytes 524800 | tf_op jit(solution)/shard_map/jit(_take)/gather | solution.py:82
  49.8 0.2 multiply_reduce_fusion.1
  50.1 0.0 collective-permute-done
  50.1 0.7 collective-permute-start.2
  50.8 0.0 collective-permute-done.1
  50.8 4.1 %collective-permute-start.3 = (bf16[64,512]{1,0:T(8,128)(2,1)S(1)}, bf16[64,512]{1,0:T(8,128)(2,1)S(1)}, u32[]{:S(2)}, u32[]{:S(2)}) collective-permute-start(bf16[64,512]{1,0:T(8,128)(2,1)S(1)} %collective-permute-done.1), channel_id=1, source_target_pairs={{0,28},{4,0},{8,4},{12,8},{16,12},{20,16},{24,20},{28,24},{1,29},{... | collective-permute-start | bytes 196616 | tf_op jit(solution)/shard_map/ppermute | solution.py:29
  54.9 2.2 %collective-permute-done.2 = bf16[64,512]{1,0:T(8,128)(2,1)S(1)} collective-permute-done((bf16[64,512]{1,0:T(8,128)(2,1)S(1)}, bf16[64,512]{1,0:T(8,128)(2,1)S(1)}, u32[]{:S(2)}, u32[]{:S(2)}) %collective-permute-start.2) | collective-permute-done | bytes 65568 | tf_op jit(solution)/shard_map/ppermute | solution.py:24
  57.1 0.0 collective-permute-start.4
  57.1 0.0 collective-permute-done.3
  57.1 4.8 %collective-permute-start.5 = (bf16[64,512]{1,0:T(8,128)(2,1)S(1)}, bf16[64,512]{1,0:T(8,128)(2,1)S(1)}, u32[]{:S(2)}, u32[]{:S(2)}) collective-permute-start(bf16[64,512]{1,0:T(8,128)(2,1)S(1)} %collective-permute-done.3), channel_id=1, source_target_pairs={{0,28},{4,0},{8,4},{12,8},{16,12},{20,16},{24,20},{28,24},{1,29},{... | collective-permute-start | bytes 196616 | tf_op jit(solution)/shard_map/ppermute | solution.py:29
  62.0 2.7 %collective-permute-done.4 = bf16[64,512]{1,0:T(8,128)(2,1)S(1)} collective-permute-done((bf16[64,512]{1,0:T(8,128)(2,1)S(1)}, bf16[64,512]{1,0:T(8,128)(2,1)S(1)}, u32[]{:S(2)}, u32[]{:S(2)}) %collective-permute-start.4) | collective-permute-done | bytes 65568 | tf_op jit(solution)/shard_map/ppermute | solution.py:24
  64.7 0.0 collective-permute-start.6
  64.7 0.0 collective-permute-done.5
  64.7 6.9 %collective-permute-done.6 = bf16[64,512]{1,0:T(8,128)(2,1)S(1)} collective-permute-done((bf16[64,512]{1,0:T(8,128)(2,1)S(1)}, bf16[64,512]{1,0:T(8,128)(2,1)S(1)}, u32[]{:S(2)}, u32[]{:S(2)}) %collective-permute-start.6) | collective-permute-done | bytes 65568 | tf_op jit(solution)/shard_map/ppermute | solution.py:24
  71.6 0.4 fusion.1
  72.0 17.1 %all-reduce.1 = (f32[512]{0:T(512)S(1)}, f32[512]{0:T(512)S(1)}) all-reduce(f32[512]{0:T(512)S(1)} %get-tuple-element.46, f32[512]{0:T(512)S(1)} %get-tuple-element.45), channel_id=1, replica_groups=mesh['center'=8,'rep'=4] {'center'}, use_global_device_ids=true, to_apply=%region_13.15 | all-reduce | flops 1024 | bytes 8192 | tf_op jit(solution)/shard_map/psum | solution.py:108
  89.2 1.0 fusion.14
  90.2 0.0 copy-start.1
  90.2 0.0 all-reduce.6.cloned.1.call-update
  90.2 0.0 reduce-scatter.2.cloned.1.call-start
  90.2 1.4 fusion.4
  91.6 0.0 reduce-scatter.2.cloned.1.call-update
  91.7 3.1 %gather_fusion.1 = f32[128,512]{1,0:T(8,128)S(1)} fusion(f32[2048,512]{1,0:T(8,128)} %param.20, s32[1024]{0:T(1024)S(1)} %pad_clamp_fusion), kind=kCustom, calls=%fused_computation.1.clone | custom fusion | bytes 524800 | tf_op jit(solution)/shard_map/jit(_take)/gather | solution.py:83
  94.8 0.6 dynamic_slice.19
  95.4 25.0 %all-reduce.6.cloned.1.call-done = f32[128,512]{1,0:T(8,128)} async-done(((f32[128,512]{1,0:T(8,128)}), f32[128,512]{1,0:T(8,128)}) %all-reduce.6.cloned.1.call-update) | async-done | bytes 262160 | tf_op jit(solution)/shard_map/psum | solution.py:138
  120.4 1.1 multiply_reduce_fusion
  121.5 2.0 %subtract_select_fusion = (f32[128,512]{1,0:T(8,128)}, f32[128,512]{1,0:T(8,128)}) fusion(f32[128,512]{1,0:T(8,128)S(1)} %gather_fusion, pred[128]{0:T(512)(128)(4,1)S(1)} %get-tuple-element.88, pred[128]{0:T(512)(128)(4,1)S(1)} %get-tuple-element.89, f32[128,512]{1,0:T(8,128)} %all-reduce.6.cloned.1.call-done, f32[128]{0:T(128)S(1)} %multiply_reduce_fusion, ...), kind=kLoop, calls=%fused_computation.4 | loop fusion | flops 917504 | bytes 1312000 | tf_op jit(solution)/shard_map/jit(_where)/select_n | solution.py:48
  123.5 33.0 %reduce-scatter.2.cloned.1.call-done = f32[64,512]{1,0:T(8,128)} async-done(((f32[512,512]{1,0:T(8,128)}), f32[64,512]{1,0:T(8,128)}) %reduce-scatter.2.cloned.1.call-update) | async-done | bytes 131088 | tf_op jit(solution)/shard_map/reduce_scatter | solution.py:133
  156.5 0.0 copy-done.1
  156.5 1.1 multiply_reduce_fusion.2
  157.6 1.7 subtract_divide_fusion
  (16 shorter events, 0.2 us)
Async XLA Ops:
  8.0 1.0 copy-start
  8.0 112.4 %all-reduce.6.cloned.1.call-start = ((), (), s32[]{:S(2)}) async-start(), calls=%async_computation.2 | async-start | bytes 524288 | tf_op jit(solution)/shard_map/psum | solution.py:138
  27.2 22.8 %collective-permute-start = (bf16[64,512]{1,0:T(8,128)(2,1)S(1)}, bf16[64,512]{1,0:T(8,128)(2,1)S(1)}, u32[]{:S(2)}, u32[]{:S(2)}) collective-permute-start(bf16[64,512]{1,0:T(8,128)(2,1)S(1)} %get-tuple-element.80), channel_id=1, source_target_pairs={{0,4},{4,8},{8,12},{12,16},{16,20},{20,24},{24,28},{28,0},{1,5},{5... | collective-permute-start | bytes 196616 | tf_op jit(solution)/shard_map/ppermute | solution.py:24
  28.9 21.8 %collective-permute-start.1 = (bf16[64,512]{1,0:T(8,128)(2,1)S(1)}, bf16[64,512]{1,0:T(8,128)(2,1)S(1)}, u32[]{:S(2)}, u32[]{:S(2)}) collective-permute-start(bf16[64,512]{1,0:T(8,128)(2,1)S(1)} %get-tuple-element.80), channel_id=1, source_target_pairs={{0,28},{4,0},{8,4},{12,8},{16,12},{20,16},{24,20},{28,24},{1,29},{... | collective-permute-start | bytes 196616 | tf_op jit(solution)/shard_map/ppermute | solution.py:29
  50.1 7.0 %collective-permute-start.2 = (bf16[64,512]{1,0:T(8,128)(2,1)S(1)}, bf16[64,512]{1,0:T(8,128)(2,1)S(1)}, u32[]{:S(2)}, u32[]{:S(2)}) collective-permute-start(bf16[64,512]{1,0:T(8,128)(2,1)S(1)} %collective-permute-done), channel_id=1, source_target_pairs={{0,4},{4,8},{8,12},{12,16},{16,20},{20,24},{24,28},{28,0},{1,5},{5... | collective-permute-start | bytes 196616 | tf_op jit(solution)/shard_map/ppermute | solution.py:24
  50.8 6.3 %collective-permute-start.3 = (bf16[64,512]{1,0:T(8,128)(2,1)S(1)}, bf16[64,512]{1,0:T(8,128)(2,1)S(1)}, u32[]{:S(2)}, u32[]{:S(2)}) collective-permute-start(bf16[64,512]{1,0:T(8,128)(2,1)S(1)} %collective-permute-done.1), channel_id=1, source_target_pairs={{0,28},{4,0},{8,4},{12,8},{16,12},{20,16},{24,20},{28,24},{1,29},{... | collective-permute-start | bytes 196616 | tf_op jit(solution)/shard_map/ppermute | solution.py:29
  57.1 7.6 %collective-permute-start.4 = (bf16[64,512]{1,0:T(8,128)(2,1)S(1)}, bf16[64,512]{1,0:T(8,128)(2,1)S(1)}, u32[]{:S(2)}, u32[]{:S(2)}) collective-permute-start(bf16[64,512]{1,0:T(8,128)(2,1)S(1)} %collective-permute-done.2), channel_id=1, source_target_pairs={{0,4},{4,8},{8,12},{12,16},{16,20},{20,24},{24,28},{28,0},{1,5},{5... | collective-permute-start | bytes 196616 | tf_op jit(solution)/shard_map/ppermute | solution.py:24
  57.1 7.6 %collective-permute-start.5 = (bf16[64,512]{1,0:T(8,128)(2,1)S(1)}, bf16[64,512]{1,0:T(8,128)(2,1)S(1)}, u32[]{:S(2)}, u32[]{:S(2)}) collective-permute-start(bf16[64,512]{1,0:T(8,128)(2,1)S(1)} %collective-permute-done.3), channel_id=1, source_target_pairs={{0,28},{4,0},{8,4},{12,8},{16,12},{20,16},{24,20},{28,24},{1,29},{... | collective-permute-start | bytes 196616 | tf_op jit(solution)/shard_map/ppermute | solution.py:29
  64.7 7.0 %collective-permute-start.6 = (bf16[64,512]{1,0:T(8,128)(2,1)S(1)}, bf16[64,512]{1,0:T(8,128)(2,1)S(1)}, u32[]{:S(2)}, u32[]{:S(2)}) collective-permute-start(bf16[64,512]{1,0:T(8,128)(2,1)S(1)} %collective-permute-done.4), channel_id=1, source_target_pairs={{0,4},{4,8},{8,12},{12,16},{16,20},{20,24},{24,28},{28,0},{1,5},{5... | collective-permute-start | bytes 196616 | tf_op jit(solution)/shard_map/ppermute | solution.py:24
  90.2 66.3 %copy-start.1 = (f32[512]{0:T(512)S(1)}, f32[512]{0:T(512)}, u32[]{:S(2)}) copy-start(f32[512]{0:T(512)} %param.18) | copy-start | bytes 6148
  90.2 66.3 %reduce-scatter.2.cloned.1.call-start = ((), (), s32[]{:S(2)}) async-start(), calls=%async_computation.1 | async-start | bytes 1179648 | tf_op jit(solution)/shard_map/reduce_scatter | solution.py:133
Sparse Core Ops, SparseCore 0:
  90.3 30.0 all-reduce.5
Sparse Core Ops, SparseCore 1:
  94.1 62.3 reduce-scatter.1
